TPU v7x, 32 devices: a whole 2x2x4 slice. The times are simulated.
32 devices in a mesh: slides: 2 (over y), tiles: 4 (over z), heads: 4 (over x, core).
Axes of the slice: x: 2, y: 2, z: 4, core: 2. Of those that a mesh axis runs over, the one named last changes fastest.
Arguments:
- pixels: bfloat16 [32, 4096, 192], P(('slides', 'tiles', 'heads')), parts along dimension 0, may hold values from -6 to 6
- w_stem: bfloat16 [192, 64], replicated, may hold values from -0.4375 to 0.4375
- w_conv1: bfloat16 [4, 9, 16, 32], replicated, may hold values from -0.5 to 0.5
- w_conv2: bfloat16 [4, 9, 32, 64], replicated, may hold values from -0.375 to 0.375
- w_key: bfloat16 [256, 512], P(None, 'heads'), may hold values from -0.375 to 0.375
- w_value: bfloat16 [256, 512], P(None, 'heads'), may hold values from -0.375 to 0.375
- queries: bfloat16 [512, 512], P(None, 'heads'), may hold values from -104 to 104
- tile_count: int32 [32], P(('slides', 'tiles', 'heads')), parts along dimension 0, may hold values from 0 to 1, as said below
- tissue: int32 [32], P(('slides', 'tiles', 'heads')), parts along dimension 0, may hold values from 17 to 256, as said below
- adjacency: int32 [32, 3], P(('slides', 'tiles', 'heads')), parts along dimension 0, may hold values from -1 to 0, as said below
Outputs:
- pooled: bfloat16 [1024, 512], P(('slides', 'tiles'), 'heads'), parts along dimension 0
There are 2 independent parts, one for each index of `slides`. A program takes and returns all parts, laid end to end along the dimension named above; an argument that names none is the same for every part. Nothing has to cross between parts.
Inputs may be any that keep to these rules, and one draw needn't show every extreme that they name: Device g (order of tiles+heads) holds tiles in its slots 0 to tile_count[g] - 1; the first device holds 1, the second 1; other devices may hold none. Tokens 0 to tissue[s] - 1 of slot s, raster order, are tissue; slot 0 is all tissue. `adjacency`: A code below 1 names a slot of the previous device along tiles+heads, a code c of 1 or more names slot c - 1 of the same device, earlier than the slot itself; -1 is background.
All inputs are finite; a program needn't handle non-finite values.
Results may differ from a plain program's by a relative error of at most 0.012.
The roundings to bfloat16 on the way count: a program that leaves them out, or rounds other values in their place, can miss the bound.
Values may be sent and summed in bfloat16 or wider, within the bound.
No kernel may reach another device: no remote copies, remote signals or barrier semaphores. Data moves between devices by JAX's collectives and lax.ppermute only.
A program may use at most 128 MiB of HBM per device.

v0:
```python
import jax
import jax.numpy as jnp
from jax import lax
from jax.sharding import PartitionSpec as P

STEM_GRID = 64
PATCH_DIM = 192
C_STEM = 64
C_OUT = 256
HEAD_DIM = 64
TOK_TILE = 256
NEG_BIG = -1e30
LN_EPS = 1e-05


def passed_along(block, axis, distance):
    devices = range(lax.axis_size(axis))
    route = [(i - distance, i) for i in devices if i - distance in devices]
    return lax.ppermute(block, axis, route)


def merged_2(array, axis, combine):
    everything = jax.tree.map(lambda part: lax.all_gather(part, axis), array)
    first = jax.tree.map(lambda part: part[0], everything)

    def lap(k, so_far):
        return combine(so_far, jax.tree.map(lambda part: part[k], everything))

    return lax.fori_loop(1, lax.axis_size(axis), lap, first)


def border_lines(feature_map):
    slot_n = feature_map.shape[0]
    side = feature_map.shape[1]
    channels = feature_map.shape[3]
    return jnp.stack([feature_map[:, side - 1], feature_map[:, :, side - 1]], axis=1).reshape(
        slot_n, 2, side * channels
    )


def bordered(inner, earlier, own_lines, adjacency):
    slot_n = inner.shape[0]
    side = inner.shape[1]
    channels = inner.shape[3]
    lines = jnp.concatenate([earlier, own_lines], axis=0)
    source_n = lines.shape[0]
    chooser = (
        adjacency[:, :, None] == jnp.arange(source_n, dtype=jnp.int32)[None, None, :]
    ).astype(jnp.bfloat16)
    above = (
        jnp.dot(chooser[:, 0], lines[:, 0], preferred_element_type=jnp.float32)
        .astype(jnp.bfloat16)
        .reshape(slot_n, side, channels)
    )
    beside = (
        jnp.dot(chooser[:, 1], lines[:, 1], preferred_element_type=jnp.float32)
        .astype(jnp.bfloat16)
        .reshape(slot_n, side, channels)
    )
    last_pixel = lines[:, 0].reshape(source_n, side, channels)[:, side - 1]
    corner = jnp.dot(chooser[:, 2], last_pixel, preferred_element_type=jnp.float32).astype(
        jnp.bfloat16
    )
    first_line = jnp.concatenate([corner[:, None], above], axis=1)
    lower = jnp.concatenate([beside[:, :, None], inner], axis=2)
    return jnp.concatenate([first_line[:, None], lower], axis=1)


def grouped_conv(padded, weight):
    groups_n = weight.shape[0]
    in_group = weight.shape[2]
    out_group = weight.shape[3]
    kernel = (
        weight.reshape(groups_n, 3, 3, in_group, out_group)
        .transpose(1, 2, 3, 0, 4)
        .reshape(3, 3, in_group, groups_n * out_group)
    )
    return lax.conv_general_dilated(
        padded,
        kernel,
        window_strides=(2, 2),
        padding="VALID",
        dimension_numbers=("NHWC", "HWIO", "NHWC"),
        feature_group_count=groups_n,
        preferred_element_type=jnp.float32,
    )


def partial_attention(query_heads, key_rows, value_rows, valid_rows):
    scores = jnp.einsum(
        "lhd,thd->hlt", query_heads, key_rows, preferred_element_type=jnp.float32
    ) * float(HEAD_DIM) ** (-0.5)
    scores = jnp.where(valid_rows[None, None, :] > 0.5, scores, NEG_BIG)
    row_peak = jnp.max(scores, axis=2)
    weights = jnp.exp(scores - row_peak[:, :, None]) * valid_rows[None, None, :]
    totals = jnp.sum(weights, axis=2)
    weighted = jnp.einsum(
        "hlt,thd->lhd", weights.astype(jnp.bfloat16), value_rows, preferred_element_type=jnp.float32
    )
    latent_n = query_heads.shape[0]
    return (row_peak.T, totals.T, weighted.reshape(latent_n, -1))


def softmax_merge(first, second):
    joint = jnp.maximum(first[0], second[0])
    scale_one = jnp.exp(first[0] - joint)
    scale_two = jnp.exp(second[0] - joint)
    totals = first[1] * scale_one + second[1] * scale_two
    weighted = first[2] * jnp.repeat(scale_one, HEAD_DIM, axis=1) + second[2] * jnp.repeat(
        scale_two, HEAD_DIM, axis=1
    )
    return (joint, totals, weighted)


def per_device(
    pixels, w_stem, w_conv1, w_conv2, w_key, w_value, queries, tile_count, tissue, adjacency
):
    slot_n = pixels.shape[0]
    slot_live = (jnp.arange(slot_n, dtype=jnp.int32) < tile_count[0]).astype(jnp.float32)
    stem_flat = jnp.dot(
        pixels.reshape(slot_n * STEM_GRID * STEM_GRID, PATCH_DIM),
        w_stem,
        preferred_element_type=jnp.float32,
    )
    stem_map = (
        jnp.maximum(stem_flat, 0.0).reshape(slot_n, STEM_GRID, STEM_GRID, C_STEM)
        * slot_live[:, None, None, None]
    ).astype(jnp.bfloat16)
    stem_lines = border_lines(stem_map)
    stem_prior = passed_along(stem_lines, ("tiles", "heads"), 1)
    middle = grouped_conv(bordered(stem_map, stem_prior, stem_lines, adjacency), w_conv1)
    middle = (jnp.maximum(middle, 0.0) * slot_live[:, None, None, None]).astype(jnp.bfloat16)
    middle_lines = border_lines(middle)
    middle_prior = passed_along(middle_lines, ("tiles", "heads"), 1)
    deepest = jnp.maximum(
        grouped_conv(bordered(middle, middle_prior, middle_lines, adjacency), w_conv2), 0.0
    )
    token_n = slot_n * TOK_TILE
    deepest = deepest.reshape(token_n, C_OUT)
    centred = deepest - jnp.mean(deepest, axis=1, keepdims=True)
    normed = (
        centred * lax.rsqrt(jnp.mean(centred * centred, axis=1, keepdims=True) + LN_EPS)
    ).astype(jnp.bfloat16)
    in_tile = (jnp.arange(TOK_TILE, dtype=jnp.int32)[None, :] < tissue[:, None]).astype(jnp.float32)
    valid = (in_tile * slot_live[:, None]).reshape(token_n).astype(jnp.bfloat16)
    latent_n = queries.shape[0]
    head_local = queries.shape[1] // HEAD_DIM
    head_width = head_local * HEAD_DIM
    weight_both = jnp.concatenate([w_key, w_value], axis=1)
    query_heads = queries.reshape(latent_n, head_local, HEAD_DIM)

    def attend_rows(running, normed_rows, valid_rows):
        projected = jnp.dot(normed_rows, weight_both, preferred_element_type=jnp.float32).astype(
            jnp.bfloat16
        )
        key_rows = projected[:, :head_width].reshape(-1, head_local, HEAD_DIM)
        value_rows = projected[:, head_width:].reshape(-1, head_local, HEAD_DIM)
        return softmax_merge(
            running, partial_attention(query_heads, key_rows, value_rows, valid_rows)
        )

    start_state = (
        jnp.full((latent_n, head_local), NEG_BIG, jnp.float32),
        jnp.zeros((latent_n, head_local), jnp.float32),
        jnp.zeros((latent_n, head_width), jnp.float32),
    )
    normed_rows = lax.all_gather(normed, "heads", axis=0, tiled=True)
    valid_rows = lax.all_gather(valid, "heads", axis=0, tiled=True)
    row_total = normed_rows.shape[0]
    blocks = (
        normed_rows.reshape(row_total // token_n, token_n, C_OUT),
        valid_rows.reshape(row_total // token_n, token_n),
    )

    def scan_step(inner_state, block_pair):
        return (attend_rows(inner_state, block_pair[0], block_pair[1]), None)

    softmax_state = lax.scan(scan_step, start_state, blocks)[0]
    tile_n = lax.axis_size("tiles")
    share = latent_n // tile_n
    merged = merged_2(softmax_state, "tiles", softmax_merge)
    first_row = lax.axis_index("tiles") * share
    totals = lax.dynamic_slice_in_dim(merged[1], first_row, share, 0)
    weighted = lax.dynamic_slice_in_dim(merged[2], first_row, share, 0)
    return (weighted / jnp.repeat(totals, HEAD_DIM, axis=1)).astype(jnp.bfloat16)


def solution(mesh):
    in_specs = (
        P(("slides", "tiles", "heads"), None, None),
        P(),
        P(),
        P(),
        P(None, "heads"),
        P(None, "heads"),
        P(None, "heads"),
        P(("slides", "tiles", "heads")),
        P(("slides", "tiles", "heads")),
        P(("slides", "tiles", "heads"), None),
    )
    out_specs = P(("slides", "tiles"), "heads")
    return jax.shard_map(
        per_device, mesh=mesh, in_specs=in_specs, out_specs=out_specs, check_vma=False
    )
```

profile of v0, /device:TPU:0, one launch (start us, length us, event | category | flops | bytes accessed | tf_op | source)
XLA Modules:
  0.0 160.6 jit_solution(8616740887920046742)
XLA Ops:
  7.3 0.6 copy-done
  8.0 1.2 fusion.19
  9.2 1.1 convert_element_type.93
  10.3 1.4 slice.83
  11.7 2.4 %copy.115 = bf16[1,64,1,64]{3,1,2,0:T(8,128)(2,1)S(1)} copy(bf16[1,64,1,64]{2,1,3,0:T(8,128)(2,1)} %slice.83) | data formatting | bytes 16384
  14.5 2.4 %collective-permute-start = (bf16[1,2,4096]{2,1,0:T(2,128)(2,1)S(1)}, bf16[1,2,4096]{2,1,0:T(2,128)(2,1)S(1)}, u32[]{:S(2)}, u32[]{:S(2)}) collective-permute-start(bf16[1,2,4096]{2,1,0:T(2,128)(2,1)S(1)} %pad_maximum_fusion.2), channel_id=1, source_target_pairs={{0,1},{1,2},{2,3},{3,4},{4,5},{5,6},{6,7},{7,8},{8,9},{9,10},{10,1... | collective-permute-start | bytes 49160 | tf_op jit(solution)/shard_map/ppermute | solution.py:19
  16.9 2.1 %convert_element_type.97 = bf16[1,64,64,4,16]{2,1,4,3,0:T(8,128)(2,1)} reshape(bf16[4096,64]{0,1:T(8,128)(2,1)S(1)} %fusion.19) | data formatting | bytes 1048576 | tf_op jit(solution)/shard_map/convert_element_type | solution.py:128
  19.1 2.9 %copy.91 = bf16[1,64,64,4,16]{2,4,3,1,0:T(8,128)(2,1)} copy(bf16[1,64,64,4,16]{2,1,4,3,0:T(8,128)(2,1)} %convert_element_type.97) | data formatting | bytes 1048576 | tf_op jit(solution)/shard_map/convert_element_type | solution.py:128
  23.0 3.2 %concatenate.63 = bf16[1,64,1,4,16]{2,4,3,1,0:T(8,128)(2,1)} reshape(bf16[4096]{0:T(1024)(128)(2,1)S(1)} %convert_element_type.96) | data formatting | bytes 16384 | tf_op jit(solution)/shard_map/concatenate | solution.py:65
  26.9 2.1 %maximum_maximum_fusion.1 = bf16[1,65,65,4,16]{2,4,3,1,0:T(8,128)(2,1)S(1)} fusion(bf16[1,64,64,4,16]{2,4,3,1,0:T(8,128)(2,1)} %copy.91, bf16[1,64,1,4,16]{2,4,3,1,0:T(8,128)(2,1)} %concatenate.63, bf16[1,1,64,4,16]{2,4,3,1,0:T(8,128)(2,1)S(1)} %copy.89, bf16[1,1,1,4,16]{2,4,3,1,0:T(8,128)(2,1)S(1)} %concatenate.62), kind=kLoop, calls=%fused_computation.51 | loop fusion | flops 2163200 | bytes 1081600 | tf_op jit(solution)/shard_map/concatenate | solution.py:66
  29.0 13.2 %copy.92 = bf16[1,65,65,4,16]{4,0,3,2,1:T(2,128)(2,1)} copy(bf16[1,65,65,4,16]{2,4,3,1,0:T(8,128)(2,1)S(1)} %maximum_maximum_fusion.1) | data formatting | bytes 1081600 | tf_op jit(solution)/shard_map/concatenate | solution.py:66
  42.2 22.5 %fusion.39 = (bf16[32,32,4,32]{3,2,1,0:T(4,128)(2,1)S(1)}, bf16[1,32,32,4,32]{4,0,3,2,1:T(2,128)(2,1)}) fusion(f32[]{:T(128)} %bitcast.6, bf16[1,65,65,4,16]{4,0,3,2,1:T(2,128)(2,1)} %copy.92, bf16[4,3,3,16,32]{4,3,2,1,0:T(8,128)(2,1)S(1)} %bitcast.205), kind=kOutput, calls=%fused_computation.90 | convolution fusion | flops 38141952 | bytes 1101956 | tf_op jit(solution)/shard_map/conv_general_dilated | solution.py:78
  64.7 0.5 convert_element_type.99
  65.3 4.5 %collective-permute-start.1 = (bf16[1,2,4096]{2,0,1:T(2,128)(2,1)S(1)}, bf16[1,2,4096]{2,0,1:T(2,128)(2,1)S(1)}, u32[]{:S(2)}, u32[]{:S(2)}) collective-permute-start(bf16[1,2,4096]{2,0,1:T(2,128)(2,1)S(1)} %pad_maximum_fusion.1), channel_id=1, source_target_pairs={{0,1},{1,2},{2,3},{3,4},{4,5},{5,6},{6,7},{7,8},{8,9},{9,10},{10,1... | collective-permute-start | bytes 49160 | tf_op jit(solution)/shard_map/ppermute | solution.py:19
  69.9 5.1 %all-gather.3 = bf16[4,1,256]{2,1,0:T(2,128)(2,1)S(1)} all-gather(bf16[1,1,256]{2,1,0:T(2,128)(2,1)S(1)} %reshape.325), channel_id=1, replica_groups=mesh['slides'=2,'tiles'=4,'heads'=4] {'heads'}, dimensions={0}, use_global_device_ids=true | all-gather | bytes 2560 | tf_op jit(solution)/shard_map/all_gather | solution.py:168
  75.1 5.2 %copy.99 = bf16[1,32,32,4,32]{2,4,3,1,0:T(8,128)(2,1)S(1)} copy(bf16[1,32,32,4,32]{4,0,3,2,1:T(2,128)(2,1)} %get-tuple-element.341) | data formatting | bytes 524288 | tf_op jit(solution)/shard_map/convert_element_type | solution.py:132
  80.8 3.1 %concatenate.65 = bf16[1,32,1,4,32]{2,4,3,1,0:T(8,128)(2,1)} reshape(bf16[4096]{0:T(1024)(128)(2,1)S(1)} %convert_element_type.102) | data formatting | bytes 16384 | tf_op jit(solution)/shard_map/concatenate | solution.py:65
  84.2 0.2 concatenate.64
  84.5 2.8 %maximum_maximum_fusion = bf16[1,33,33,4,32]{2,4,3,1,0:T(8,128)(2,1)} fusion(bf16[1,32,32,4,32]{2,4,3,1,0:T(8,128)(2,1)S(1)} %copy.99, bf16[1,32,1,4,32]{2,4,3,1,0:T(8,128)(2,1)} %concatenate.65, bf16[1,1,32,4,32]{2,4,3,1,0:T(8,128)(2,1)S(1)} %copy.97, bf16[1,1,1,4,32]{2,4,3,1,0:T(8,128)(2,1)S(1)} %concatenate.64), kind=kLoop, calls=%fused_computation.50 | loop fusion | flops 1115136 | bytes 557568 | tf_op jit(solution)/shard_map/concatenate | solution.py:66
  87.3 6.1 %copy.100 = bf16[1,33,33,4,32]{4,0,3,2,1:T(2,128)(2,1)} copy(bf16[1,33,33,4,32]{2,4,3,1,0:T(8,128)(2,1)} %maximum_maximum_fusion) | data formatting | bytes 557568 | tf_op jit(solution)/shard_map/concatenate | solution.py:66
  93.4 5.4 %fusion.40 = (f32[16,16]{1,0:T(8,128)S(1)}, f32[1,16,16,4,64]{4,0,3,2,1:T(1,128)S(1)}) fusion(bf16[1,33,33,4,32]{4,0,3,2,1:T(2,128)(2,1)} %copy.100, bf16[4,3,3,32,64]{4,3,2,1,0:T(8,128)(2,1)S(1)} %bitcast.204), kind=kOutput, calls=%fused_computation.91 | convolution fusion | flops 37879552 | bytes 689408 | tf_op jit(solution)/shard_map/conv_general_dilated | solution.py:78
  99.0 0.5 broadcast.180
  99.5 3.4 %multiply_reduce_fusion = (f32[16,16]{1,0:T(8,128)S(1)}, f32[16,16,4,64]{3,2,1,0:T(4,128)S(1)}) fusion(f32[1,16,16,4,64]{4,0,3,2,1:T(1,128)S(1)} %get-tuple-element.343, f32[16,16]{1,0:T(8,128)S(1)} %broadcast_multiply_fusion, f32[]{:T(128)} %broadcast.180), kind=kLoop, calls=%fused_computation.52 | loop fusion | flops 196352 | bytes 526340 | tf_op jit(solution)/shard_map/reduce_sum | solution.py:142
  102.9 0.3 max.55
  103.5 7.7 %all_gather.25 = bf16[1024,256]{1,0:T(8,128)(2,1)} all-gather(bf16[256,256]{1,0:T(8,128)(2,1)S(1)} %multiply_convert_fusion), channel_id=1, replica_groups=mesh['slides'=2,'tiles'=4,'heads'=4] {'heads'}, dimensions={0}, use_global_device_ids=true | all-gather | bytes 655360 | tf_op jit(solution)/shard_map/all_gather | solution.py:167
  111.2 9.0 %while.35 = (s32[]{:T(128)}, f32[512,2]{0,1:T(2,128)S(1)}, f32[512,2]{0,1:T(2,128)S(1)}, f32[512,128]{0,1:T(8,128)S(1)}, bf16[4,256]{1,0:T(4,128)(2,1)S(1)}, /*i...) while((s32[]{:T(128)}, f32[512,2]{0,1:T(2,128)S(1)}, ...), condition=%wide.region_5.6_spmd.clone, body=%wide.region_2.5_spmd.clone.sunk | while | flops 103357440 | bytes 5174392 | solution.py:178
  111.2 1.1 convolution_convert_fusion.2
  112.4 0.4 fusion.71
  113.1 0.3 fusion.75
  113.5 1.1 convolution_convert_fusion.2
  114.7 0.4 fusion.71
  115.3 0.3 fusion.75
  115.7 1.1 convolution_convert_fusion.2
  116.9 0.4 fusion.71
  117.5 0.3 fusion.75
  118.0 1.1 convolution_convert_fusion.2
  119.2 0.4 fusion.71
  119.8 0.3 fusion.75
  120.2 0.7 copy-done.1
  121.0 13.4 %all-gather = f32[2048,2]{0,1:T(2,128)S(1)} all-gather(f32[512,2]{0,1:T(2,128)S(1)} %get-tuple-element.226), channel_id=2, replica_groups=mesh['slides'=2,'tiles'=4,'heads'=4] {'tiles'}, dimensions={0}, use_global_device_ids=true | all-gather | bytes 20480 | tf_op jit(solution)/shard_map/all_gather | solution.py:23
  134.3 13.3 %all-gather.1 = f32[2048,2]{0,1:T(2,128)S(1)} all-gather(f32[512,2]{0,1:T(2,128)S(1)} %get-tuple-element.227), channel_id=3, replica_groups=mesh['slides'=2,'tiles'=4,'heads'=4] {'tiles'}, dimensions={0}, use_global_device_ids=true | all-gather | bytes 20480 | tf_op jit(solution)/shard_map/all_gather | solution.py:23
  147.6 2.1 %all-gather.6.cloned.1.call-done = f32[2048,128]{0,1:T(8,128)} async-done(((f32[512,128]{0,1:T(8,128)}), f32[2048,128]{0,1:T(8,128)}) %all-gather.6.cloned.1.call-update) | async-done | bytes 1048592 | tf_op jit(solution)/shard_map/all_gather | solution.py:23
  149.7 2.0 %reshape.318 = f32[4,512,128]{1,0,2:T(4,128)S(1)} reshape(f32[2048,128]{0,1:T(8,128)} %all-gather.6.cloned.1.call-done) | data formatting | bytes 2097152 | tf_op jit(solution)/shard_map/all_gather | solution.py:23
  151.7 1.2 while.34
  151.8 0.2 constant_dynamic-slice_fusion.4
  152.2 0.2 constant_dynamic-slice_fusion.4
  152.6 0.2 constant_dynamic-slice_fusion.4
  153.0 0.7 copy.106
  (100 shorter events, 4.8 us)
Async XLA Ops:
  6.5 1.4 copy-start
  6.5 143.2 %all-gather.6.cloned.1.call-start = ((), (), s32[]{:S(2)}) async-start(), calls=%async_computation | async-start | bytes 1310720 | tf_op jit(solution)/shard_map/all_gather | solution.py:23
  9.1 7.7 %copy-start.7 = (s32[1,3]{1,0:T(1,128)S(1)}, s32[1,3]{1,0:T(1,128)}, u32[]{:S(2)}) copy-start(s32[1,3]{1,0:T(1,128)} %param.23) | copy-start | bytes 40
  9.1 7.8 %copy-start.3 = (bf16[256,128]{1,0:T(8,128)(2,1)S(1)}, bf16[256,128]{1,0:T(8,128)(2,1)}, u32[]{:S(2)}) copy-start(bf16[256,128]{1,0:T(8,128)(2,1)} %param.19) | copy-start | bytes 196612
  9.2 7.8 %copy-start.4 = (bf16[256,128]{1,0:T(8,128)(2,1)S(1)}, bf16[256,128]{1,0:T(8,128)(2,1)}, u32[]{:S(2)}) copy-start(bf16[256,128]{1,0:T(8,128)(2,1)} %param.18) | copy-start | bytes 196612
  14.5 8.1 %collective-permute-start = (bf16[1,2,4096]{2,1,0:T(2,128)(2,1)S(1)}, bf16[1,2,4096]{2,1,0:T(2,128)(2,1)S(1)}, u32[]{:S(2)}, u32[]{:S(2)}) collective-permute-start(bf16[1,2,4096]{2,1,0:T(2,128)(2,1)S(1)} %pad_maximum_fusion.2), channel_id=1, source_target_pairs={{0,1},{1,2},{2,3},{3,4},{4,5},{5,6},{6,7},{7,8},{8,9},{9,10},{10,1... | collective-permute-start | bytes 49160 | tf_op jit(solution)/shard_map/ppermute | solution.py:19
  29.0 13.2 %copy-start.6 = (bf16[4,9,16,32]{3,2,1,0:T(8,128)(2,1)S(1)}, bf16[4,9,16,32]{3,2,1,0:T(8,128)(2,1)}, u32[]{:S(2)}) copy-start(bf16[4,9,16,32]{3,2,1,0:T(8,128)(2,1)} %param.16) | copy-start | bytes 110596
  42.2 32.7 %copy-start.2 = (bf16[512,128]{1,0:T(8,128)(2,1)S(1)}, bf16[512,128]{1,0:T(8,128)(2,1)}, u32[]{:S(2)}) copy-start(bf16[512,128]{1,0:T(8,128)(2,1)} %param.20) | copy-start | bytes 393220
  65.3 15.0 %collective-permute-start.1 = (bf16[1,2,4096]{2,0,1:T(2,128)(2,1)S(1)}, bf16[1,2,4096]{2,0,1:T(2,128)(2,1)S(1)}, u32[]{:S(2)}, u32[]{:S(2)}) collective-permute-start(bf16[1,2,4096]{2,0,1:T(2,128)(2,1)S(1)} %pad_maximum_fusion.1), channel_id=1, source_target_pairs={{0,1},{1,2},{2,3},{3,4},{4,5},{5,6},{6,7},{7,8},{8,9},{9,10},{10,1... | collective-permute-start | bytes 49160 | tf_op jit(solution)/shard_map/ppermute | solution.py:19
  87.3 6.1 %copy-start.5 = (bf16[4,9,32,64]{3,2,1,0:T(8,128)(2,1)S(1)}, bf16[4,9,32,64]{3,2,1,0:T(8,128)(2,1)}, u32[]{:S(2)}) copy-start(bf16[4,9,32,64]{3,2,1,0:T(8,128)(2,1)} %param.17) | copy-start | bytes 442372
  120.2 0.7 copy-start.1
  149.7 2.0 %slice-start = ((f32[2048,128]{0,1:T(8,128)}), f32[512,128]{0,1:T(8,128)S(1)}, s32[]{:S(2)}) async-start(f32[2048,128]{0,1:T(8,128)} %all-gather.6.cloned.1.call-done), calls=%async_computation.1 | async-start | bytes 524288 | tf_op jit(solution)/shard_map/slice | solution.py:24
Sparse Core Ops, SparseCore 0:
  121.1 28.5 all-gather.5
where the time goes:
time: 161 us
  local copies, waits for them, and re-layouts  48.7 us (30%)
  blocking collectives  39.4 us (24%)
  matrix products  37.1 us (23%)
  between operations  15.2 us (9%)
  other arithmetic  10.8 us (7%)
  starting transfers between devices  6.87 us (4%)
  waiting for transfers between devices  2.12 us (1%)
    conv_general_dilated x2, matrix products, grouped_conv(): lax.conv_general_dilated(padded, kernel, window_strides=(2, 2), padding='...  27.9 us
    all_gather x2, blocking collectives, merged_2(): everything = jax.tree.map(lambda part: lax.all_gather(part, axis), array)  26.6 us
    concatenate x2, local copies, waits for them, and re-layouts, bordered(): return jnp.concatenate([first_line[:, None], lower], axis=1)  19.3 us
    all_gather x1, blocking collectives, per_device(): normed_rows = lax.all_gather(normed, 'heads', axis=0, tiled=True)  7.71 us
    ppermute x2, starting transfers between devices, passed_along(): return lax.ppermute(block, axis, route)  6.87 us
    concatenate x2, local copies, waits for them, and re-layouts, bordered(): lower = jnp.concatenate([beside[:, :, None], inner], axis=2)  6.28 us
    convert_element_type x3, local copies, waits for them, and re-layouts, per_device(): stem_map = (jnp.maximum(stem_flat, 0.0).reshape(slot_n, STEM_GRID, STEM_G...  6.14 us
    convert_element_type x2, local copies, waits for them, and re-layouts, per_device(): (jnp.maximum(middle, 0.0) * slot_live[:, None, None, None]).astype(jnp.bf...  5.74 us
  transfers between devices with their start and end apart: 3, of which 1 were waited for; matrix products, arithmetic and copies ran while one was open for 7% of the time, Pallas kernels for 0%

commit v1 on v0

--- a/solution.py
+++ b/solution.py
@@ -164,7 +164,15 @@
         jnp.zeros((latent_n, head_local), jnp.float32),
         jnp.zeros((latent_n, head_width), jnp.float32),
     )
-    normed_rows = lax.all_gather(normed, "heads", axis=0, tiled=True)
+    ways, here, lap_2 = (lax.axis_size("heads"), lax.axis_index("heads"), normed.shape[0])
+    line, have = (normed, 1)
+    while have < ways:
+        line = jnp.concatenate(
+            [line, lax.ppermute(line, "heads", [(d, (d - have) % ways) for d in range(ways)])],
+            axis=0,
+        )
+        have = 2 * have
+    normed_rows = jnp.roll(line, here * lap_2, axis=0)
     valid_rows = lax.all_gather(valid, "heads", axis=0, tiled=True)
     row_total = normed_rows.shape[0]
     blocks = (

time: 161 us -> 163 us (1.012)
  blocking collectives: 39.4 us -> 36.1 us
  starting transfers between devices: 6.87 us -> 9.27 us
  local copies, waits for them, and re-layouts: 48.7 us -> 50.5 us
    all_gather x1 -> x0, blocking collectives: 7.71 us -> none  [per_device(): normed_rows = lax.all_gather(normed, 'heads', axis=0, tiled=True)]
    all_gather x1, blocking collectives: 5.07 us -> 9.53 us  [per_device(): valid_rows = lax.all_gather(valid, 'heads', axis=0, tiled=True)]
    unnamed x23 -> x27, local copies, waits for them, and re-layouts: 4.03 us -> 6.71 us
    ppermute x0 -> x2, starting transfers between devices: none -> 2.4 us  [per_device(): lax.ppermute(line, 'heads', [(d, (d - have) % ways) for d in range(ways)])]
    convert_element_type x3, local copies, waits for them, and re-layouts: 6.14 us -> 3.9 us  [per_device(): stem_map = (jnp.maximum(stem_flat, 0.0).reshape(slot_n, STEM_GRID, STEM_G...]
    dynamic_slice x0 -> x1, local copies, waits for them, and re-layouts: none -> 1.88 us  [per_device(): normed_rows = jnp.roll(line, here * lap_2, axis=0)]
    ppermute x0 -> x2, waiting for transfers between devices: none -> 1.87 us  [per_device(): lax.ppermute(line, 'heads', [(d, (d - have) % ways) for d in range(ways)])]
  transfers between devices with their start and end apart: 3 -> 5, of which waited for: 1 -> 2; matrix products, arithmetic and copies ran while one was open for 7% -> 6% of each run, Pallas kernels for 0% -> 0%
where the time goes in v1:
time: 163 us; the launch traced here: 162 us
  local copies, waits for them, and re-layouts  50.5 us (31%)
  matrix products  37.1 us (23%)
  blocking collectives  36.1 us (22%)
  between operations  15.3 us (9%)
  other arithmetic  10.8 us (7%)
  starting transfers between devices  9.27 us (6%)
  waiting for transfers between devices  3.06 us (2%)
    conv_general_dilated x2, matrix products, grouped_conv(): lax.conv_general_dilated(padded, kernel, window_strides=(2, 2), padding='...  27.9 us
    all_gather x2, blocking collectives, merged_2(): everything = jax.tree.map(lambda part: lax.all_gather(part, axis), array)  26.6 us
    concatenate x2, local copies, waits for them, and re-layouts, bordered(): return jnp.concatenate([first_line[:, None], lower], axis=1)  17.9 us
    all_gather x1, blocking collectives, per_device(): valid_rows = lax.all_gather(valid, 'heads', axis=0, tiled=True)  9.53 us
    ppermute x2, starting transfers between devices, passed_along(): return lax.ppermute(block, axis, route)  6.87 us
    unnamed x27, local copies, waits for them, and re-layouts  6.71 us
    concatenate x2, local copies, waits for them, and re-layouts, bordered(): lower = jnp.concatenate([beside[:, :, None], inner], axis=2)  6.25 us
    convert_element_type x2, local copies, waits for them, and re-layouts, per_device(): (jnp.maximum(middle, 0.0) * slot_live[:, None, None, None]).astype(jnp.bf...  6.06 us
  transfers between devices with their start and end apart: 5, of which 2 were waited for; matrix products, arithmetic and copies ran while one was open for 6% of the time, Pallas kernels for 0%

profile of v1, /device:TPU:0, one launch (start us, length us, event | category | flops | bytes accessed | tf_op | source)
XLA Modules:
  0.0 162.4 jit_solution(240375965372454754)
XLA Ops:
  7.3 0.6 copy-done
  8.0 1.2 fusion.19
  9.1 1.1 convert_element_type.93
  10.3 1.4 slice.83
  11.7 2.4 %copy.115 = bf16[1,64,1,64]{3,1,2,0:T(8,128)(2,1)S(1)} copy(bf16[1,64,1,64]{2,1,3,0:T(8,128)(2,1)} %slice.83) | data formatting | bytes 16384
  14.4 2.4 %collective-permute-start = (bf16[1,2,4096]{2,1,0:T(2,128)(2,1)S(1)}, bf16[1,2,4096]{2,1,0:T(2,128)(2,1)S(1)}, u32[]{:S(2)}, u32[]{:S(2)}) collective-permute-start(bf16[1,2,4096]{2,1,0:T(2,128)(2,1)S(1)} %pad_maximum_fusion.3), channel_id=1, source_target_pairs={{0,1},{1,2},{2,3},{3,4},{4,5},{5,6},{6,7},{7,8},{8,9},{9,10},{10,1... | collective-permute-start | bytes 49160 | tf_op jit(solution)/shard_map/ppermute | solution.py:19
  16.9 1.1 convert_element_type.97
  18.0 1.6 %copy.91 = bf16[1,64,64,4,16]{2,4,3,1,0:T(8,128)(2,1)} copy(bf16[1,64,64,4,16]{2,1,4,3,0:T(8,128)(2,1)S(1)} %convert_element_type.97) | data formatting | bytes 1048576 | tf_op jit(solution)/shard_map/convert_element_type | solution.py:128
  20.0 3.2 %concatenate.75 = bf16[1,64,1,4,16]{2,4,3,1,0:T(8,128)(2,1)} reshape(bf16[4096]{0:T(1024)(128)(2,1)S(1)} %convert_element_type.96) | data formatting | bytes 16384 | tf_op jit(solution)/shard_map/concatenate | solution.py:65
  23.9 2.1 %maximum_maximum_fusion.1 = bf16[1,65,65,4,16]{2,4,3,1,0:T(8,128)(2,1)S(1)} fusion(bf16[1,64,64,4,16]{2,4,3,1,0:T(8,128)(2,1)} %copy.91, bf16[1,64,1,4,16]{2,4,3,1,0:T(8,128)(2,1)} %concatenate.75, bf16[1,1,64,4,16]{2,4,3,1,0:T(8,128)(2,1)S(1)} %copy.89, bf16[1,1,1,4,16]{2,4,3,1,0:T(8,128)(2,1)S(1)} %concatenate.74), kind=kLoop, calls=%fused_computation.51 | loop fusion | flops 2163200 | bytes 1081600 | tf_op jit(solution)/shard_map/concatenate | solution.py:66
  26.1 13.1 %copy.92 = bf16[1,65,65,4,16]{4,0,3,2,1:T(2,128)(2,1)} copy(bf16[1,65,65,4,16]{2,4,3,1,0:T(8,128)(2,1)S(1)} %maximum_maximum_fusion.1) | data formatting | bytes 1081600 | tf_op jit(solution)/shard_map/concatenate | solution.py:66
  39.2 22.4 %fusion.39 = (bf16[32,32,4,32]{3,2,1,0:T(4,128)(2,1)S(1)}, bf16[1,32,32,4,32]{4,0,3,2,1:T(2,128)(2,1)}) fusion(f32[]{:T(128)} %bitcast.6, bf16[1,65,65,4,16]{4,0,3,2,1:T(2,128)(2,1)} %copy.92, bf16[4,3,3,16,32]{4,3,2,1,0:T(8,128)(2,1)S(1)} %bitcast.205), kind=kOutput, calls=%fused_computation.98 | convolution fusion | flops 38141952 | bytes 1101956 | tf_op jit(solution)/shard_map/conv_general_dilated | solution.py:78
  61.6 0.5 convert_element_type.99
  62.2 4.5 %collective-permute-start.1 = (bf16[1,2,4096]{2,0,1:T(2,128)(2,1)S(1)}, bf16[1,2,4096]{2,0,1:T(2,128)(2,1)S(1)}, u32[]{:S(2)}, u32[]{:S(2)}) collective-permute-start(bf16[1,2,4096]{2,0,1:T(2,128)(2,1)S(1)} %pad_maximum_fusion.2), channel_id=1, source_target_pairs={{0,1},{1,2},{2,3},{3,4},{4,5},{5,6},{6,7},{7,8},{8,9},{9,10},{10,1... | collective-permute-start | bytes 49160 | tf_op jit(solution)/shard_map/ppermute | solution.py:19
  66.7 5.6 %copy.99 = bf16[1,32,32,4,32]{2,4,3,1,0:T(8,128)(2,1)} copy(bf16[1,32,32,4,32]{4,0,3,2,1:T(2,128)(2,1)} %get-tuple-element.343) | data formatting | bytes 524288 | tf_op jit(solution)/shard_map/convert_element_type | solution.py:132
  72.7 3.1 %concatenate.77 = bf16[1,32,1,4,32]{2,4,3,1,0:T(8,128)(2,1)} reshape(bf16[4096]{0:T(1024)(128)(2,1)S(1)} %convert_element_type.102) | data formatting | bytes 16384 | tf_op jit(solution)/shard_map/concatenate | solution.py:65
  76.4 2.1 %maximum_maximum_fusion = bf16[1,33,33,4,32]{2,4,3,1,0:T(8,128)(2,1)S(1)} fusion(bf16[1,32,32,4,32]{2,4,3,1,0:T(8,128)(2,1)} %copy.99, bf16[1,32,1,4,32]{2,4,3,1,0:T(8,128)(2,1)} %concatenate.77, bf16[1,1,32,4,32]{2,4,3,1,0:T(8,128)(2,1)S(1)} %copy.97, bf16[1,1,1,4,32]{2,4,3,1,0:T(8,128)(2,1)S(1)} %concatenate.76), kind=kLoop, calls=%fused_computation.50 | loop fusion | flops 1115136 | bytes 557568 | tf_op jit(solution)/shard_map/concatenate | solution.py:66
  78.5 4.8 %copy.100 = bf16[1,33,33,4,32]{4,0,3,2,1:T(2,128)(2,1)} copy(bf16[1,33,33,4,32]{2,4,3,1,0:T(8,128)(2,1)S(1)} %maximum_maximum_fusion) | data formatting | bytes 557568 | tf_op jit(solution)/shard_map/concatenate | solution.py:66
  83.3 5.4 %fusion.40 = (f32[16,16]{1,0:T(8,128)S(1)}, f32[1,16,16,4,64]{4,0,3,2,1:T(1,128)S(1)}) fusion(bf16[1,33,33,4,32]{4,0,3,2,1:T(2,128)(2,1)} %copy.100, bf16[4,3,3,32,64]{4,3,2,1,0:T(8,128)(2,1)S(1)} %bitcast.204), kind=kOutput, calls=%fused_computation.99 | convolution fusion | flops 37879552 | bytes 689408 | tf_op jit(solution)/shard_map/conv_general_dilated | solution.py:78
  88.9 0.5 broadcast.181
  89.4 3.4 %multiply_reduce_fusion = (f32[16,16]{1,0:T(8,128)S(1)}, f32[16,16,4,64]{3,2,1,0:T(4,128)S(1)}) fusion(f32[1,16,16,4,64]{4,0,3,2,1:T(1,128)S(1)} %get-tuple-element.345, f32[16,16]{1,0:T(8,128)S(1)} %broadcast_multiply_fusion, f32[]{:T(128)} %broadcast.181), kind=kLoop, calls=%fused_computation.52 | loop fusion | flops 196352 | bytes 526340 | tf_op jit(solution)/shard_map/reduce_sum | solution.py:142
  92.8 0.3 max.55
  93.3 0.8 constant_dynamic-update-slice_fusion.5
  94.0 2.3 %collective-permute-start.2 = (bf16[256,256]{1,0:T(8,128)(2,1)S(1)}, bf16[256,256]{1,0:T(8,128)(2,1)S(1)}, u32[]{:S(2)}, u32[]{:S(2)}) collective-permute-start(bf16[256,256]{1,0:T(8,128)(2,1)S(1)} %get-tuple-element.334), channel_id=1, source_target_pairs={{0,3},{1,0},{2,1},{3,2},{4,7},{5,4},{6,5},{7,6},{8,11},{9,8},{10,9... | collective-permute-start | bytes 393224 | tf_op jit(solution)/shard_map/ppermute | solution.py:171
  97.0 1.9 %collective-permute-done.2 = bf16[256,256]{1,0:T(8,128)(2,1)S(1)} collective-permute-done((bf16[256,256]{1,0:T(8,128)(2,1)S(1)}, bf16[256,256]{1,0:T(8,128)(2,1)S(1)}, u32[]{:S(2)}, u32[]{:S(2)}) %collective-permute-start.2) | collective-permute-done | bytes 131104 | tf_op jit(solution)/shard_map/ppermute | solution.py:171
  99.1 9.5 %all-gather.3 = bf16[4,1,256]{2,1,0:T(2,128)(2,1)S(1)} all-gather(bf16[1,1,256]{2,1,0:T(2,128)(2,1)S(1)} %reshape.325), channel_id=1, replica_groups=mesh['slides'=2,'tiles'=4,'heads'=4] {'heads'}, dimensions={0}, use_global_device_ids=true | all-gather | bytes 2560 | tf_op jit(solution)/shard_map/all_gather | solution.py:176
  108.8 0.7 constant_dynamic-update-slice_fusion.4
  109.5 0.7 constant_dynamic-update-slice_fusion.3
  110.2 0.7 constant_dynamic-update-slice_fusion.2
  110.8 0.7 constant_dynamic-update-slice_fusion.1
  111.5 0.7 constant_dynamic-update-slice_fusion
  112.2 1.9 %constant_dynamic-slice_fusion.3 = bf16[1024,256]{1,0:T(8,128)(2,1)} fusion(bf16[2048,256]{1,0:T(8,128)(2,1)} %constant_dynamic-update-slice_fusion, s32[]{:T(128)S(6)} %select_n.37), kind=kLoop, calls=%fused_computation.92 | loop fusion | bytes 1048580 | tf_op jit(solution)/shard_map/jit(_roll_dynamic)/dynamic_slice | solution.py:175
  114.1 9.0 %while.35 = (s32[]{:T(128)}, f32[512,2]{0,1:T(2,128)S(1)}, f32[512,2]{0,1:T(2,128)S(1)}, f32[512,128]{0,1:T(8,128)S(1)}, bf16[4,256]{1,0:T(4,128)(2,1)S(1)}, /*i...) while((s32[]{:T(128)}, f32[512,2]{0,1:T(2,128)S(1)}, ...), condition=%wide.region_5.6_spmd.clone, body=%wide.region_2.5_spmd.clone.sunk | while | flops 103357440 | bytes 5174392 | solution.py:186
  114.1 1.1 convolution_convert_fusion.2
  115.3 0.4 fusion.71
  116.3 1.1 convolution_convert_fusion.2
  117.5 0.4 fusion.71
  118.6 1.1 convolution_convert_fusion.2
  119.8 0.4 fusion.71
  120.8 1.1 convolution_convert_fusion.2
  122.0 0.4 fusion.71
  123.1 0.7 copy-done.1
  123.8 13.4 %all-gather = f32[2048,2]{0,1:T(2,128)S(1)} all-gather(f32[512,2]{0,1:T(2,128)S(1)} %get-tuple-element.226), channel_id=2, replica_groups=mesh['slides'=2,'tiles'=4,'heads'=4] {'tiles'}, dimensions={0}, use_global_device_ids=true | all-gather | bytes 20480 | tf_op jit(solution)/shard_map/all_gather | solution.py:23
  137.2 13.2 %all-gather.1 = f32[2048,2]{0,1:T(2,128)S(1)} all-gather(f32[512,2]{0,1:T(2,128)S(1)} %get-tuple-element.227), channel_id=3, replica_groups=mesh['slides'=2,'tiles'=4,'heads'=4] {'tiles'}, dimensions={0}, use_global_device_ids=true | all-gather | bytes 20480 | tf_op jit(solution)/shard_map/all_gather | solution.py:23
  150.4 1.2 all-gather.6.cloned.1.call-done
  151.6 2.0 %reshape.318 = f32[4,512,128]{1,0,2:T(4,128)S(1)} reshape(f32[2048,128]{0,1:T(8,128)} %all-gather.6.cloned.1.call-done) | data formatting | bytes 2097152 | tf_op jit(solution)/shard_map/all_gather | solution.py:23
  153.6 1.2 while.34
  154.9 0.7 copy.106
  (110 shorter events, 6.9 us)
Async XLA Ops:
  6.5 1.4 copy-start
  6.5 145.0 %all-gather.6.cloned.1.call-start = ((), (), s32[]{:S(2)}) async-start(), calls=%async_computation | async-start | bytes 1310720 | tf_op jit(solution)/shard_map/all_gather | solution.py:23
  9.1 7.7 %copy-start.7 = (s32[1,3]{1,0:T(1,128)S(1)}, s32[1,3]{1,0:T(1,128)}, u32[]{:S(2)}) copy-start(s32[1,3]{1,0:T(1,128)} %param.23) | copy-start | bytes 40
  14.4 5.2 %collective-permute-start = (bf16[1,2,4096]{2,1,0:T(2,128)(2,1)S(1)}, bf16[1,2,4096]{2,1,0:T(2,128)(2,1)S(1)}, u32[]{:S(2)}, u32[]{:S(2)}) collective-permute-start(bf16[1,2,4096]{2,1,0:T(2,128)(2,1)S(1)} %pad_maximum_fusion.3), channel_id=1, source_target_pairs={{0,1},{1,2},{2,3},{3,4},{4,5},{5,6},{6,7},{7,8},{8,9},{9,10},{10,1... | collective-permute-start | bytes 49160 | tf_op jit(solution)/shard_map/ppermute | solution.py:19
  26.0 13.1 %copy-start.6 = (bf16[4,9,16,32]{3,2,1,0:T(8,128)(2,1)S(1)}, bf16[4,9,16,32]{3,2,1,0:T(8,128)(2,1)}, u32[]{:S(2)}) copy-start(bf16[4,9,16,32]{3,2,1,0:T(8,128)(2,1)} %param.16) | copy-start | bytes 110596
  62.2 10.1 %collective-permute-start.1 = (bf16[1,2,4096]{2,0,1:T(2,128)(2,1)S(1)}, bf16[1,2,4096]{2,0,1:T(2,128)(2,1)S(1)}, u32[]{:S(2)}, u32[]{:S(2)}) collective-permute-start(bf16[1,2,4096]{2,0,1:T(2,128)(2,1)S(1)} %pad_maximum_fusion.2), channel_id=1, source_target_pairs={{0,1},{1,2},{2,3},{3,4},{4,5},{5,6},{6,7},{7,8},{8,9},{9,10},{10,1... | collective-permute-start | bytes 49160 | tf_op jit(solution)/shard_map/ppermute | solution.py:19
  78.5 4.8 %copy-start.5 = (bf16[4,9,32,64]{3,2,1,0:T(8,128)(2,1)S(1)}, bf16[4,9,32,64]{3,2,1,0:T(8,128)(2,1)}, u32[]{:S(2)}) copy-start(bf16[4,9,32,64]{3,2,1,0:T(8,128)(2,1)} %param.17) | copy-start | bytes 442372
  88.7 19.9 %copy-start.2 = (bf16[512,128]{1,0:T(8,128)(2,1)S(1)}, bf16[512,128]{1,0:T(8,128)(2,1)}, u32[]{:S(2)}) copy-start(bf16[512,128]{1,0:T(8,128)(2,1)} %param.20) | copy-start | bytes 393220
  88.8 20.0 %copy-start.3 = (bf16[256,128]{1,0:T(8,128)(2,1)S(1)}, bf16[256,128]{1,0:T(8,128)(2,1)}, u32[]{:S(2)}) copy-start(bf16[256,128]{1,0:T(8,128)(2,1)} %param.19) | copy-start | bytes 196612
  88.8 20.0 %copy-start.4 = (bf16[256,128]{1,0:T(8,128)(2,1)S(1)}, bf16[256,128]{1,0:T(8,128)(2,1)}, u32[]{:S(2)}) copy-start(bf16[256,128]{1,0:T(8,128)(2,1)} %param.18) | copy-start | bytes 196612
  94.0 4.9 %collective-permute-start.2 = (bf16[256,256]{1,0:T(8,128)(2,1)S(1)}, bf16[256,256]{1,0:T(8,128)(2,1)S(1)}, u32[]{:S(2)}, u32[]{:S(2)}) collective-permute-start(bf16[256,256]{1,0:T(8,128)(2,1)S(1)} %get-tuple-element.334), channel_id=1, source_target_pairs={{0,3},{1,0},{2,1},{3,2},{4,7},{5,4},{6,5},{7,6},{8,11},{9,8},{10,9... | collective-permute-start | bytes 393224 | tf_op jit(solution)/shard_map/ppermute | solution.py:171
  98.9 10.5 %collective-permute-start.3 = (bf16[512,256]{1,0:T(8,128)(2,1)S(1)}, bf16[512,256]{1,0:T(8,128)(2,1)S(1)}, u32[]{:S(2)}, u32[]{:S(2)}) collective-permute-start(bf16[512,256]{1,0:T(8,128)(2,1)S(1)} %pad_maximum_fusion), channel_id=1, source_target_pairs={{0,2},{1,3},{2,0},{3,1},{4,6},{5,7},{6,4},{7,5},{8,10},{9,11},{10,... | collective-permute-start | bytes 786440 | tf_op jit(solution)/shard_map/ppermute | solution.py:171
  123.1 0.7 copy-start.1
  151.6 2.0 %slice-start = ((f32[2048,128]{0,1:T(8,128)}), f32[512,128]{0,1:T(8,128)S(1)}, s32[]{:S(2)}) async-start(f32[2048,128]{0,1:T(8,128)} %all-gather.6.cloned.1.call-done), calls=%async_computation.1 | async-start | bytes 524288 | tf_op jit(solution)/shard_map/slice | solution.py:24
Sparse Core Ops, SparseCore 0:
  123.9 27.6 all-gather.5
